TPU v7x, 128 devices: a whole 4x4x4 slice. The times are simulated.
128 devices in a mesh: rows: 32 (over y_hi, z, x), batch: 4 (over y_lo, core).
Axes of the slice: x: 4, y: 4 (y_hi: 2, y_lo: 2; y = y_hi * 2 + y_lo), z: 4, core: 2. Of those that a mesh axis runs over, the one named last changes fastest.
Arguments:
- features: bfloat16 [4, 256, 128, 256], P('batch', 'rows'), may hold values from -6 to 6
- kernels: bfloat16 [3, 3, 3, 256, 256], replicated, may hold values from -0.125 to 0.125
- cotangent: bfloat16 [4, 256, 128, 256], P('batch', 'rows'), may hold values from -6 to 6
Outputs:
- result: bfloat16 [4, 256, 128, 256], P('batch', 'rows')
- grad_features: bfloat16 [4, 256, 128, 256], P('batch', 'rows')
- grad_kernels: float32 [3, 3, 3, 256, 256], replicated
All inputs are finite; a program needn't handle non-finite values.
Results may differ from a plain program's by a relative error of at most 0.0065.
Values may be sent and summed in bfloat16 or wider, within the bound.
No kernel may reach another device: no remote copies, remote signals or barrier semaphores. Data moves between devices by JAX's collectives and lax.ppermute only.
A program may use at most 128 MiB of HBM per device.

v0:
```python
import math
import jax
import jax.numpy as jnp
from jax import lax
from jax.sharding import PartitionSpec as P


def passed_along(value, axis, steps):
    count = lax.axis_size(axis)
    initial, last = (max(0, -steps), min(count, count - steps))
    return lax.ppermute(value, axis, [(source, source + steps) for source in range(initial, last)])


def activate(values):
    values = values.astype(jnp.float32)
    normed = values * lax.rsqrt(jnp.mean(values * values, axis=-1, keepdims=True) + 1e-05)
    return normed * jax.nn.sigmoid(normed)


def shift_columns(array, offset):
    width = array.shape[2]
    reach = abs(offset)
    padded = jnp.pad(array, ((0, 0), (0, 0), (reach, reach), (0, 0)))
    return padded[:, :, reach + offset : reach + offset + width]


def tap_forward(source, kernel_row, dilation):
    channels = kernel_row.shape[1]
    widened = jnp.transpose(kernel_row, (1, 0, 2)).reshape(channels, 3 * channels)
    product = jnp.einsum("shwc,cd->shwd", source, widened, preferred_element_type=jnp.float32)
    total = shift_columns(product[..., 0:channels], -dilation)
    total = total + product[..., channels : 2 * channels]
    return total + shift_columns(product[..., 2 * channels :], dilation)


def tap_backward(source, kernel_row, dilation):
    channels = kernel_row.shape[1]
    widened = jnp.transpose(kernel_row, (2, 0, 1)).reshape(channels, 3 * channels)
    product = jnp.einsum("shwd,dc->shwc", source, widened, preferred_element_type=jnp.float32)
    total = shift_columns(product[..., 0:channels], dilation)
    total = total + product[..., channels : 2 * channels]
    return total + shift_columns(product[..., 2 * channels :], -dilation)


def kernel_terms(source, grad_flow, dilation):
    channels = grad_flow.shape[3]
    stacked = jnp.concatenate(
        [shift_columns(grad_flow, dilation), grad_flow, shift_columns(grad_flow, -dilation)], axis=3
    )
    terms = jnp.einsum("shwc,shwd->cd", source, stacked, preferred_element_type=jnp.float32)
    return jnp.transpose(terms.reshape(channels, 3, channels), (1, 0, 2))


def fetch_bands(signal, bands_away):
    upper_band = passed_along(signal, "rows", bands_away)
    lower_band = passed_along(signal, "rows", -bands_away)
    return (upper_band, lower_band)


def fetch_grads(grad_flow, bands_away):
    grad_upper = passed_along(grad_flow, "rows", bands_away)
    grad_lower = passed_along(grad_flow, "rows", -bands_away)
    return (grad_upper, grad_lower)


def local(features, kernels, cotangent):
    band_rows = features.shape[1]
    count = lax.axis_size("rows")
    spans = [4, 8, 16]
    current = features
    grad_flow = cotangent
    saved = []
    for layer in range(3):
        dilation = spans[layer] * band_rows
        signal = activate(current).astype(jnp.bfloat16)
        upper_band, lower_band = fetch_bands(signal, spans[layer])
        conv_out = tap_forward(signal, kernels[layer, 1], dilation)
        conv_out = conv_out + tap_forward(upper_band, kernels[layer, 0], dilation)
        conv_out = conv_out + tap_forward(lower_band, kernels[layer, 2], dilation)
        saved.append((current, signal, upper_band, lower_band))
        current = (current.astype(jnp.float32) + conv_out).astype(jnp.bfloat16)
    pixel_count = features.shape[0] * band_rows * features.shape[2] * count * lax.axis_size("batch")
    factor = 1.0 / math.sqrt(pixel_count)
    kernel_grads = [None, None, None]
    for layer in [2, 1, 0]:
        dilation = spans[layer] * band_rows
        layer_input, signal, upper_band, lower_band = saved[layer]
        grad_upper, grad_lower = fetch_grads(grad_flow, spans[layer])
        dsignal = tap_backward(grad_flow, kernels[layer, 1], dilation)
        dsignal = dsignal + tap_backward(grad_lower, kernels[layer, 0], dilation)
        dsignal = dsignal + tap_backward(grad_upper, kernels[layer, 2], dilation)
        local_grad = (
            jnp.stack(
                [
                    kernel_terms(upper_band, grad_flow, dilation),
                    kernel_terms(signal, grad_flow, dilation),
                    kernel_terms(lower_band, grad_flow, dilation),
                ]
            )
            * factor
        )
        kernel_grads[layer] = local_grad
        _, back = jax.vjp(activate, layer_input.astype(jnp.float32))
        (dinput,) = back(dsignal)
        grad_flow = (grad_flow.astype(jnp.float32) + dinput).astype(jnp.bfloat16)
    summed = lax.psum(jnp.stack(kernel_grads), ("rows", "batch"))
    return (current, grad_flow, summed)


def solution(mesh):
    placed = (P("batch", "rows", None, None), P(), P("batch", "rows", None, None))
    return jax.shard_map(
        local,
        mesh=mesh,
        in_specs=placed,
        out_specs=(P("batch", "rows", None, None), P("batch", "rows", None, None), P()),
        check_vma=False,
    )
```

profile of v0, /device:TPU:1, one launch (start us, length us, event | category | flops | bytes accessed | tf_op | source)
XLA Modules:
  0.0 324.4 jit_solution(16525500430960883256)
XLA Ops:
  7.2 1.3 fusion.58
  8.5 2.2 fusion.33
  10.7 1.3 collective-permute-start.1
  12.0 5.8 %collective-permute-start = (bf16[1,8,128,256]{3,2,1,0:T(8,128)(2,1)}, bf16[1,8,128,256]{3,2,1,0:T(8,128)(2,1)}, u32[]{:S(2)}, u32[]{:S(2)}) collective-permute-start(bf16[1,8,128,256]{3,2,1,0:T(8,128)(2,1)} %fusion.33), channel_id=1, source_target_pairs={{0,16},{4,20},{8,24},{12,28},{16,32},{20,36},{24,40},{28,44},{32,4... | collective-permute-start | bytes 1572872 | tf_op jit(solution)/shard_map/ppermute | solution.py:11
  17.8 6.7 %collective-permute-start.7 = (bf16[1,8,128,256]{3,2,1,0:T(8,128)(2,1)}, bf16[1,8,128,256]{3,2,1,0:T(8,128)(2,1)}, u32[]{:S(2)}, u32[]{:S(2)}) collective-permute-start(bf16[1,8,128,256]{3,2,1,0:T(8,128)(2,1)} %param.5), channel_id=1, source_target_pairs={{0,64},{4,68},{8,72},{12,76},{16,80},{20,84},{24,88},{28,92},{32,9... | collective-permute-start | bytes 1572872 | tf_op jit(solution)/shard_map/ppermute | solution.py:11
  24.5 1.3 collective-permute-start.6
  25.8 3.5 %fusion.118 = (bf16[1,1,3,256,256]{4,3,2,1,0:T(8,128)(2,1)}, bf16[1,1,3,256,256]{4,3,2,1,0:T(8,128)(2,1)}, bf16[1,1,3,256,256]{4,3,2,1,0:T(8,128)(2,1)}, bf16[1,...) fusion(bf16[3,3,3,256,256]{4,3,2,1,0:T(8,128)(2,1)} %param.4), kind=kLoop, calls=%fused_computation.206 | loop fusion | bytes 7077888 | tf_op jit(solution)/shard_map/slice | solution.py:77
  29.3 0.9 copy.159
  30.2 1.8 convolution_bitcast_fusion.17
  32.1 2.7 convolution_bitcast_fusion.8
  34.8 2.1 copy.89
  36.9 1.6 fusion.128
  38.6 1.4 pad_maximum_fusion.1
  40.0 0.9 copy.164
  42.4 1.6 convolution_bitcast_fusion.15
  44.2 1.6 convolution_bitcast_fusion.16
  47.6 1.8 fusion.60
  49.8 1.3 collective-permute-start.3
  51.1 5.5 %collective-permute-start.2 = (bf16[1,8,128,256]{3,2,1,0:T(8,128)(2,1)S(1)}, bf16[1,8,128,256]{3,2,1,0:T(8,128)(2,1)S(1)}, u32[]{:S(2)}, u32[]{:S(2)}) collective-permute-start(bf16[1,8,128,256]{3,2,1,0:T(8,128)(2,1)S(1)} %fusion.27), channel_id=1, source_target_pairs={{0,32},{4,36},{8,40},{12,44},{16,48},{20,52},{24,56},{28,60},{32,6... | collective-permute-start | bytes 1572872 | tf_op jit(solution)/shard_map/ppermute | solution.py:11
  57.2 1.6 convolution_bitcast_fusion.6
  59.9 1.6 convolution_bitcast_fusion.7
  61.5 3.9 %collective-permute-done.3 = bf16[1,8,128,256]{3,2,1,0:T(8,128)(2,1)S(1)} collective-permute-done((bf16[1,8,128,256]{3,2,1,0:T(8,128)(2,1)S(1)}, bf16[1,8,128,256]{3,2,1,0:T(8,128)(2,1)S(1)}, u32[]{:S(2)}, u32[]{:S(2)}) %collective-permute-start.3) | collective-permute-done | bytes 524320 | tf_op jit(solution)/shard_map/ppermute | solution.py:11
  66.2 13.0 %collective-permute-done.2 = bf16[1,8,128,256]{3,2,1,0:T(8,128)(2,1)S(1)} collective-permute-done((bf16[1,8,128,256]{3,2,1,0:T(8,128)(2,1)S(1)}, bf16[1,8,128,256]{3,2,1,0:T(8,128)(2,1)S(1)}, u32[]{:S(2)}, u32[]{:S(2)}) %collective-permute-start.2) | collective-permute-done | bytes 524320 | tf_op jit(solution)/shard_map/ppermute | solution.py:11
  80.6 2.1 fusion.73
  82.7 1.4 fusion.45
  84.1 1.3 collective-permute-start.5
  85.4 7.1 %collective-permute-start.4 = (bf16[1,8,128,256]{3,2,1,0:T(8,128)(2,1)}, bf16[1,8,128,256]{3,2,1,0:T(8,128)(2,1)}, u32[]{:S(2)}, u32[]{:S(2)}) collective-permute-start(bf16[1,8,128,256]{3,2,1,0:T(8,128)(2,1)} %get-tuple-element.47), channel_id=1, source_target_pairs={{0,64},{4,68},{8,72},{12,76},{16,80},{20,84},{24,88},{28,92},{32,9... | collective-permute-start | bytes 1572872 | tf_op jit(solution)/shard_map/ppermute | solution.py:11
  92.5 6.4 %collective-permute-start.9 = (bf16[1,8,128,256]{3,2,1,0:T(8,128)(2,1)S(1)}, bf16[1,8,128,256]{3,2,1,0:T(8,128)(2,1)}, u32[]{:S(2)}, u32[]{:S(2)}) collective-permute-start(bf16[1,8,128,256]{3,2,1,0:T(8,128)(2,1)S(1)} %get-tuple-element.46), channel_id=1, source_target_pairs={{0,32},{4,36},{8,40},{12,44},{16,48},{20,52},{24,56},{28,60},{32,6... | collective-permute-start | bytes 1572872 | tf_op jit(solution)/shard_map/ppermute | solution.py:11
  98.9 1.5 collective-permute-start.8
  100.5 2.3 convolution_bitcast_fusion.5
  102.8 2.5 convolution_bitcast_fusion.19
  105.3 1.3 maximum_bitcast_fusion.1
  106.6 3.0 copy.82
  109.6 3.1 convolution_bitcast_fusion.22
  112.7 1.5 convolution_bitcast_fusion.21
  115.9 1.5 convolution_bitcast_fusion.23
  117.5 2.1 collective-permute-done.9
  119.5 1.6 convolution_bitcast_fusion.3
  122.2 1.6 convolution_bitcast_fusion.4
  124.0 1.0 fusion.62
  125.6 1.3 maximum_bitcast_fusion
  126.8 2.9 copy.75
  129.7 2.3 convolution_bitcast_fusion.25
  132.0 1.7 convolution_bitcast_fusion.18
  133.7 1.7 convolution_bitcast_fusion.20
  135.7 1.2 copy-done.26
  136.9 1.7 convolution_bitcast_fusion.24
  138.6 1.8 convolution_bitcast_fusion.26
  140.9 3.4 %pad_maximum_fusion = f32[3,3,3,256,256]{4,3,2,1,0:T(8,128)} fusion(f32[1,3,3,256,256]{4,3,2,1,0:T(8,128)S(1)} %maximum_multiply_fusion.2, f32[1,3,3,256,256]{4,3,2,1,0:T(8,128)S(1)} %get-tuple-element.53, f32[1,3,3,256,256]{4,3,2,1,0:T(8,128)S(1)} %get-tuple-element.52), kind=kLoop, calls=%fused_computation | loop fusion | flops 3538944 | bytes 14155776 | tf_op jit(solution)/shard_map/stack | solution.py:106
  144.4 2.0 copy.167
  146.4 0.9 copy.166
  147.3 0.9 copy.165
  148.2 1.8 convolution_bitcast_fusion.11
  150.0 1.6 collective-permute-start.11
  151.6 1.5 collective-permute-start.10
  154.9 1.7 convolution_bitcast_fusion.9
  156.6 1.6 convolution_bitcast_fusion.10
  158.2 1.1 fusion.72
  159.4 5.4 %collective-permute-done.11 = bf16[1,8,128,256]{3,2,1,0:T(8,128)(2,1)S(1)} collective-permute-done((bf16[1,8,128,256]{3,2,1,0:T(8,128)(2,1)S(1)}, bf16[1,8,128,256]{3,2,1,0:T(8,128)(2,1)S(1)}, u32[]{:S(2)}, u32[]{:S(2)}) %collective-permute-start.11) | collective-permute-done | bytes 524320 | tf_op jit(solution)/shard_map/ppermute | solution.py:11
  165.3 5.2 %collective-permute-done.10 = bf16[1,8,128,256]{3,2,1,0:T(8,128)(2,1)S(1)} collective-permute-done((bf16[1,8,128,256]{3,2,1,0:T(8,128)(2,1)S(1)}, bf16[1,8,128,256]{3,2,1,0:T(8,128)(2,1)S(1)}, u32[]{:S(2)}, u32[]{:S(2)}) %collective-permute-start.10) | collective-permute-done | bytes 524320 | tf_op jit(solution)/shard_map/ppermute | solution.py:11
  171.5 1.1 fusion.59
  172.6 1.2 fusion.57
  173.8 137.1 %all-reduce.28.cloned.1.call-done = f32[3,3,3,256,256]{4,3,2,1,0:T(8,128)} async-done(((f32[3,3,3,256,256]{4,3,2,1,0:T(8,128)}), f32[3,3,3,256,256]{4,3,2,1,0:T(8,128)}) %all-reduce.28.cloned.1.call-update) | async-done | bytes 7077904 | tf_op jit(solution)/shard_map/psum | solution.py:106
  310.8 6.7 %copy.196 = f32[3,3,3,256,256]{4,3,2,1,0:T(8,128)} copy(f32[3,3,3,256,256]{4,3,2,1,0:T(8,128)} %all-reduce.28.cloned.1.call-done) | data formatting | bytes 14155776
  (123 shorter events, 15.0 us)
Async XLA Ops:
  7.2 303.7 %all-reduce.28.cloned.1.call-start = ((), (), s32[]{:S(2)}) async-start(), calls=%async_computation | async-start | bytes 14155776 | tf_op jit(solution)/shard_map/psum | solution.py:106
  10.7 31.7 %collective-permute-start.1 = (bf16[1,8,128,256]{3,2,1,0:T(8,128)(2,1)}, bf16[1,8,128,256]{3,2,1,0:T(8,128)(2,1)}, u32[]{:S(2)}, u32[]{:S(2)}) collective-permute-start(bf16[1,8,128,256]{3,2,1,0:T(8,128)(2,1)} %fusion.33), channel_id=1, source_target_pairs={{16,0},{20,4},{24,8},{28,12},{32,16},{36,20},{40,24},{44,28},{48,3... | collective-permute-start | bytes 1572872 | tf_op jit(solution)/shard_map/ppermute | solution.py:11
  12.0 32.3 %collective-permute-start = (bf16[1,8,128,256]{3,2,1,0:T(8,128)(2,1)}, bf16[1,8,128,256]{3,2,1,0:T(8,128)(2,1)}, u32[]{:S(2)}, u32[]{:S(2)}) collective-permute-start(bf16[1,8,128,256]{3,2,1,0:T(8,128)(2,1)} %fusion.33), channel_id=1, source_target_pairs={{0,16},{4,20},{8,24},{12,28},{16,32},{20,36},{24,40},{28,44},{32,4... | collective-permute-start | bytes 1572872 | tf_op jit(solution)/shard_map/ppermute | solution.py:11
  17.8 39.4 %collective-permute-start.7 = (bf16[1,8,128,256]{3,2,1,0:T(8,128)(2,1)}, bf16[1,8,128,256]{3,2,1,0:T(8,128)(2,1)}, u32[]{:S(2)}, u32[]{:S(2)}) collective-permute-start(bf16[1,8,128,256]{3,2,1,0:T(8,128)(2,1)} %param.5), channel_id=1, source_target_pairs={{0,64},{4,68},{8,72},{12,76},{16,80},{20,84},{24,88},{28,92},{32,9... | collective-permute-start | bytes 1572872 | tf_op jit(solution)/shard_map/ppermute | solution.py:11
  24.5 34.6 %collective-permute-start.6 = (bf16[1,8,128,256]{3,2,1,0:T(8,128)(2,1)}, bf16[1,8,128,256]{3,2,1,0:T(8,128)(2,1)}, u32[]{:S(2)}, u32[]{:S(2)}) collective-permute-start(bf16[1,8,128,256]{3,2,1,0:T(8,128)(2,1)} %param.5), channel_id=1, source_target_pairs={{64,0},{68,4},{72,8},{76,12},{80,16},{84,20},{88,24},{92,28},{96,3... | collective-permute-start | bytes 1572872 | tf_op jit(solution)/shard_map/ppermute | solution.py:11
  29.3 0.9 copy-start.8
  30.2 1.9 copy-start.3
  30.2 1.9 copy-start.10
  32.0 4.9 %copy-start.2 = (f32[1,8,128,768]{3,2,1,0:T(8,128)}, f32[1,8,128,768]{3,2,1,0:T(8,128)S(1)}, u32[]{:S(2)}) copy-start(f32[1,8,128,768]{3,2,1,0:T(8,128)S(1)} %convolution_bitcast_fusion.17) | copy-start | bytes 9437188
  36.9 1.7 copy-start.21
  38.5 1.5 copy-start.17
  38.5 2.4 copy-start.7
  38.6 2.7 copy-start.15
  38.6 3.6 %copy-start.19 = (bf16[1,1,3,256,256]{4,3,2,1,0:T(8,128)(2,1)S(1)}, bf16[1,1,3,256,256]{4,3,2,1,0:T(8,128)(2,1)}, u32[]{:S(2)}) copy-start(bf16[1,1,3,256,256]{4,3,2,1,0:T(8,128)(2,1)} %get-tuple-element.17) | copy-start | bytes 1179652
  45.9 1.0 copy-start
  45.9 1.4 copy-start.5
  45.9 1.7 copy-start.6
  49.4 7.9 %copy-start.14 = (bf16[1,1,3,256,256]{4,3,2,1,0:T(8,128)(2,1)S(1)}, bf16[1,1,3,256,256]{4,3,2,1,0:T(8,128)(2,1)}, u32[]{:S(2)}) copy-start(bf16[1,1,3,256,256]{4,3,2,1,0:T(8,128)(2,1)} %get-tuple-element.21) | copy-start | bytes 1179652
  49.7 9.1 %copy-start.22 = (bf16[1,8,128,256]{3,2,1,0:T(8,128)(2,1)}, bf16[1,8,128,256]{3,2,1,0:T(8,128)(2,1)S(1)}, u32[]{:S(2)}) copy-start(bf16[1,8,128,256]{3,2,1,0:T(8,128)(2,1)S(1)} %fusion.27) | copy-start | bytes 1572868
  49.8 15.7 %collective-permute-start.3 = (bf16[1,8,128,256]{3,2,1,0:T(8,128)(2,1)S(1)}, bf16[1,8,128,256]{3,2,1,0:T(8,128)(2,1)S(1)}, u32[]{:S(2)}, u32[]{:S(2)}) collective-permute-start(bf16[1,8,128,256]{3,2,1,0:T(8,128)(2,1)S(1)} %fusion.27), channel_id=1, source_target_pairs={{32,0},{36,4},{40,8},{44,12},{48,16},{52,20},{56,24},{60,28},{64,3... | collective-permute-start | bytes 1572872 | tf_op jit(solution)/shard_map/ppermute | solution.py:11
  51.1 28.2 %collective-permute-start.2 = (bf16[1,8,128,256]{3,2,1,0:T(8,128)(2,1)S(1)}, bf16[1,8,128,256]{3,2,1,0:T(8,128)(2,1)S(1)}, u32[]{:S(2)}, u32[]{:S(2)}) collective-permute-start(bf16[1,8,128,256]{3,2,1,0:T(8,128)(2,1)S(1)} %fusion.27), channel_id=1, source_target_pairs={{0,32},{4,36},{8,40},{12,44},{16,48},{20,52},{24,56},{28,60},{32,6... | collective-permute-start | bytes 1572872 | tf_op jit(solution)/shard_map/ppermute | solution.py:11
  58.9 1.0 copy-start.12
  59.0 6.4 %copy-start.29 = (bf16[1,1,3,256,256]{3,4,2,1,0:T(8,128)(2,1)S(1)}, bf16[1,1,3,256,256]{3,4,2,1,0:T(8,128)(2,1)}, u32[]{:S(2)}) copy-start(bf16[1,1,3,256,256]{3,4,2,1,0:T(8,128)(2,1)} %copy.164) | copy-start | bytes 1179652
  65.4 0.8 copy-start.38
  66.0 13.2 %copy-start.28 = (bf16[1,1,3,256,256]{3,4,2,1,0:T(8,128)(2,1)S(1)}, bf16[1,1,3,256,256]{3,4,2,1,0:T(8,128)(2,1)}, u32[]{:S(2)}) copy-start(bf16[1,1,3,256,256]{3,4,2,1,0:T(8,128)(2,1)} %copy.163) | copy-start | bytes 1179652
  79.3 0.8 copy-start.36
  80.6 2.1 copy-start.4
  82.7 17.7 %copy-start.20 = (bf16[1,1,3,256,256]{4,3,2,1,0:T(8,128)(2,1)S(1)}, bf16[1,1,3,256,256]{4,3,2,1,0:T(8,128)(2,1)}, u32[]{:S(2)}) copy-start(bf16[1,1,3,256,256]{4,3,2,1,0:T(8,128)(2,1)} %get-tuple-element.17) | copy-start | bytes 1179652
  84.1 47.9 %collective-permute-start.5 = (bf16[1,8,128,256]{3,2,1,0:T(8,128)(2,1)}, bf16[1,8,128,256]{3,2,1,0:T(8,128)(2,1)}, u32[]{:S(2)}, u32[]{:S(2)}) collective-permute-start(bf16[1,8,128,256]{3,2,1,0:T(8,128)(2,1)} %get-tuple-element.47), channel_id=1, source_target_pairs={{64,0},{68,4},{72,8},{76,12},{80,16},{84,20},{88,24},{92,28},{96,3... | collective-permute-start | bytes 1572872 | tf_op jit(solution)/shard_map/ppermute | solution.py:11
  85.4 48.3 %collective-permute-start.4 = (bf16[1,8,128,256]{3,2,1,0:T(8,128)(2,1)}, bf16[1,8,128,256]{3,2,1,0:T(8,128)(2,1)}, u32[]{:S(2)}, u32[]{:S(2)}) collective-permute-start(bf16[1,8,128,256]{3,2,1,0:T(8,128)(2,1)} %get-tuple-element.47), channel_id=1, source_target_pairs={{0,64},{4,68},{8,72},{12,76},{16,80},{20,84},{24,88},{28,92},{32,9... | collective-permute-start | bytes 1572872 | tf_op jit(solution)/shard_map/ppermute | solution.py:11
  92.5 27.0 %collective-permute-start.9 = (bf16[1,8,128,256]{3,2,1,0:T(8,128)(2,1)S(1)}, bf16[1,8,128,256]{3,2,1,0:T(8,128)(2,1)}, u32[]{:S(2)}, u32[]{:S(2)}) collective-permute-start(bf16[1,8,128,256]{3,2,1,0:T(8,128)(2,1)S(1)} %get-tuple-element.46), channel_id=1, source_target_pairs={{0,32},{4,36},{8,40},{12,44},{16,48},{20,52},{24,56},{28,60},{32,6... | collective-permute-start | bytes 1572872 | tf_op jit(solution)/shard_map/ppermute | solution.py:11
  98.9 22.5 %collective-permute-start.8 = (bf16[1,8,128,256]{3,2,1,0:T(8,128)(2,1)S(1)}, bf16[1,8,128,256]{3,2,1,0:T(8,128)(2,1)}, u32[]{:S(2)}, u32[]{:S(2)}) collective-permute-start(bf16[1,8,128,256]{3,2,1,0:T(8,128)(2,1)S(1)} %get-tuple-element.46), channel_id=1, source_target_pairs={{32,0},{36,4},{40,8},{44,12},{48,16},{52,20},{56,24},{60,28},{64,3... | collective-permute-start | bytes 1572872 | tf_op jit(solution)/shard_map/ppermute | solution.py:11
  100.4 2.3 copy-start.24
  106.6 3.0 copy-start.23
  109.6 3.1 copy-start.27
  109.6 3.1 copy-start.39
  112.7 2.2 copy-start.1
  114.9 1.0 copy-start.37
  115.9 3.6 %copy-start.18 = (bf16[1,1,3,256,256]{4,3,2,1,0:T(8,128)(2,1)S(1)}, bf16[1,1,3,256,256]{4,3,2,1,0:T(8,128)(2,1)}, u32[]{:S(2)}) copy-start(bf16[1,1,3,256,256]{4,3,2,1,0:T(8,128)(2,1)} %get-tuple-element.15) | copy-start | bytes 1179652
  121.2 1.0 copy-start.16
  129.7 2.3 copy-start.25
  133.7 1.8 copy-start.34
  135.5 1.4 copy-start.26
  138.6 1.9 copy-start.32
  138.6 1.9 copy-start.33
  138.6 1.9 copy-start.35
  144.4 2.0 copy-start.13
  144.4 2.9 copy-start.11
  147.3 5.9 %copy-start.9 = (bf16[1,1,3,256,256]{4,3,2,1,0:T(8,128)(2,1)S(1)}, bf16[1,1,3,256,256]{4,3,2,1,0:T(8,128)(2,1)}, u32[]{:S(2)}) copy-start(bf16[1,1,3,256,256]{4,3,2,1,0:T(8,128)(2,1)} %copy-done.8) | copy-start | bytes 1179652
  150.0 14.7 %collective-permute-start.11 = (bf16[1,8,128,256]{3,2,1,0:T(8,128)(2,1)S(1)}, bf16[1,8,128,256]{3,2,1,0:T(8,128)(2,1)S(1)}, u32[]{:S(2)}, u32[]{:S(2)}) collective-permute-start(bf16[1,8,128,256]{3,2,1,0:T(8,128)(2,1)S(1)} %fusion.47), channel_id=1, source_target_pairs={{0,16},{4,20},{8,24},{12,28},{16,32},{20,36},{24,40},{28,44},{32,4... | collective-permute-start | bytes 1572872 | tf_op jit(solution)/shard_map/ppermute | solution.py:11
  151.6 18.9 %collective-permute-start.10 = (bf16[1,8,128,256]{3,2,1,0:T(8,128)(2,1)S(1)}, bf16[1,8,128,256]{3,2,1,0:T(8,128)(2,1)S(1)}, u32[]{:S(2)}, u32[]{:S(2)}) collective-permute-start(bf16[1,8,128,256]{3,2,1,0:T(8,128)(2,1)S(1)} %fusion.47), channel_id=1, source_target_pairs={{16,0},{20,4},{24,8},{28,12},{32,16},{36,20},{40,24},{44,28},{48,3... | collective-permute-start | bytes 1572872 | tf_op jit(solution)/shard_map/ppermute | solution.py:11
  153.8 1.1 copy-start.31
  154.0 2.6 copy-start.30
Sparse Core Ops, SparseCore 0:
  144.5 166.2 all-reduce.27
where the time goes:
time: 326 us; the launch traced here: 324 us
  waiting for transfers between devices  167 us (51%)
  matrix products  43.3 us (13%)
  starting transfers between devices  41.3 us (13%)
  local copies, waits for them, and re-layouts  35.9 us (11%)
  other arithmetic  22.5 us (7%)
  between operations  14.8 us (5%)
    psum x1, waiting for transfers between devices, local(): summed = lax.psum(jnp.stack(kernel_grads), ('rows', 'batch'))  137 us
    ppermute x12, starting transfers between devices, passed_along(): lax.ppermute(value, axis, [(source, source + steps) for source in range(i...  41.3 us
    ppermute x12, waiting for transfers between devices, passed_along(): lax.ppermute(value, axis, [(source, source + steps) for source in range(i...  29.5 us
    unnamed x91, local copies, waits for them, and re-layouts  22.8 us
    dot_general x9, matrix products, kernel_terms(): jnp.einsum('shwc,shwd->cd', source, stacked, preferred_element_type=jnp.f...  17.9 us
    dot_general x9, matrix products, tap_backward(): jnp.einsum('shwd,dc->shwc', source, widened, preferred_element_type=jnp.f...  13.4 us
    dot_general x9, matrix products, tap_forward(): jnp.einsum('shwc,cd->shwd', source, widened, preferred_element_type=jnp.f...  12 us
  transfers between devices with their start and end apart: 13, of which 6 were waited for; matrix products, arithmetic and copies ran while one was open for 22% of the time, Pallas kernels for 0%

commit v1 on v0

--- a/solution.py
+++ b/solution.py
@@ -103,7 +103,9 @@
         _, back = jax.vjp(activate, layer_input.astype(jnp.float32))
         (dinput,) = back(dsignal)
         grad_flow = (grad_flow.astype(jnp.float32) + dinput).astype(jnp.bfloat16)
-    summed = lax.psum(jnp.stack(kernel_grads), ("rows", "batch"))
+    summed = jnp.stack(kernel_grads)
+    for name in ("batch", "rows"):
+        summed = lax.psum(summed, name)
     return (current, grad_flow, summed)
 
 

time: 326 us -> 683 us (2.10)
  the two profiles are of different devices: /device:TPU:1 before, /device:TPU:0 now
where the time goes in v1:
time: 683 us; the launch traced here: 681 us
  waiting for transfers between devices  521 us (76%)
  starting transfers between devices  44.5 us (7%)
  matrix products  43.2 us (6%)
  local copies, waits for them, and re-layouts  35.9 us (5%)
  other arithmetic  22.4 us (3%)
  between operations  14.8 us (2%)
    psum x2, waiting for transfers between devices, local(): summed = lax.psum(summed, name)  488 us
    ppermute x12, starting transfers between devices, passed_along(): lax.ppermute(value, axis, [(source, source + steps) for source in range(i...  44.5 us
    ppermute x12, waiting for transfers between devices, passed_along(): lax.ppermute(value, axis, [(source, source + steps) for source in range(i...  32.9 us
    unnamed x91, local copies, waits for them, and re-layouts  22.7 us
    dot_general x9, matrix products, kernel_terms(): jnp.einsum('shwc,shwd->cd', source, stacked, preferred_element_type=jnp.f...  17.8 us
  transfers between devices with their start and end apart: 14, of which 6 were waited for; matrix products, arithmetic and copies ran while one was open for 10% of the time, Pallas kernels for 0%

profile of v1, /device:TPU:0, one launch (start us, length us, event | category | flops | bytes accessed | tf_op | source)
XLA Modules:
  0.0 681.4 jit_solution(16347661668711821475)
XLA Ops:
  7.2 1.3 fusion.58
  8.5 2.2 fusion.33
  10.7 1.3 collective-permute-start.1
  12.0 5.4 collective-permute-start
  17.4 7.0 %collective-permute-start.7 = (bf16[1,8,128,256]{3,2,1,0:T(8,128)(2,1)}, bf16[1,8,128,256]{3,2,1,0:T(8,128)(2,1)}, u32[]{:S(2)}, u32[]{:S(2)}) collective-permute-start(bf16[1,8,128,256]{3,2,1,0:T(8,128)(2,1)} %param.5), channel_id=1, source_target_pairs={{0,64},{4,68},{8,72},{12,76},{16,80},{20,84},{24,88},{28,92},{32,9... | collective-permute-start | bytes 1572872 | tf_op jit(solution)/shard_map/ppermute | solution.py:11
  24.4 1.3 collective-permute-start.6
  25.7 3.5 fusion.118
  30.1 1.8 convolution_bitcast_fusion.17
  32.0 2.6 convolution_bitcast_fusion.8
  34.7 2.1 copy.89
  36.8 1.5 fusion.128
  38.4 1.4 pad_maximum_fusion.1
  39.8 0.9 copy.164
  41.1 0.9 copy.163
  42.2 1.6 convolution_bitcast_fusion.15
  44.0 1.6 convolution_bitcast_fusion.16
  47.4 1.8 fusion.60
  49.6 1.3 collective-permute-start.3
  50.9 6.1 collective-permute-start.2
  57.6 1.6 convolution_bitcast_fusion.6
  60.3 1.6 convolution_bitcast_fusion.7
  61.9 4.2 collective-permute-done.3
  66.9 11.3 %collective-permute-done.2 = bf16[1,8,128,256]{3,2,1,0:T(8,128)(2,1)S(1)} collective-permute-done((bf16[1,8,128,256]{3,2,1,0:T(8,128)(2,1)S(1)}, bf16[1,8,128,256]{3,2,1,0:T(8,128)(2,1)S(1)}, u32[]{:S(2)}, u32[]{:S(2)}) %collective-permute-start.2) | collective-permute-done | bytes 524320 | tf_op jit(solution)/shard_map/ppermute | solution.py:11
  79.6 2.1 fusion.73
  81.8 1.4 fusion.45
  83.2 1.3 collective-permute-start.5
  84.5 8.8 %collective-permute-start.4 = (bf16[1,8,128,256]{3,2,1,0:T(8,128)(2,1)}, bf16[1,8,128,256]{3,2,1,0:T(8,128)(2,1)}, u32[]{:S(2)}, u32[]{:S(2)}) collective-permute-start(bf16[1,8,128,256]{3,2,1,0:T(8,128)(2,1)} %get-tuple-element.47), channel_id=1, source_target_pairs={{0,64},{4,68},{8,72},{12,76},{16,80},{20,84},{24,88},{28,92},{32,9... | collective-permute-start | bytes 1572872 | tf_op jit(solution)/shard_map/ppermute | solution.py:11
  93.2 5.6 collective-permute-start.9
  98.8 1.5 collective-permute-start.8
  100.4 2.3 convolution_bitcast_fusion.5
  102.7 2.6 convolution_bitcast_fusion.19
  105.2 1.3 maximum_bitcast_fusion.1
  106.5 3.0 copy.82
  109.5 3.1 convolution_bitcast_fusion.22
  112.5 1.5 convolution_bitcast_fusion.21
  115.7 1.5 convolution_bitcast_fusion.23
  117.3 2.8 collective-permute-done.9
  120.0 1.6 convolution_bitcast_fusion.3
  122.7 1.7 convolution_bitcast_fusion.4
  124.5 1.0 fusion.62
  126.0 1.3 maximum_bitcast_fusion
  127.3 2.9 copy.75
  130.2 2.3 convolution_bitcast_fusion.25
  132.5 1.7 convolution_bitcast_fusion.18
  134.2 1.7 convolution_bitcast_fusion.20
  136.2 1.2 copy-done.26
  137.4 1.7 convolution_bitcast_fusion.24
  139.1 1.8 convolution_bitcast_fusion.26
  141.4 3.4 pad_maximum_fusion
  144.9 138.3 %all-reduce.29.cloned.1.call-done = f32[3,3,3,256,256]{4,3,2,1,0:T(8,128)} async-done(((f32[3,3,3,256,256]{4,3,2,1,0:T(8,128)}), f32[3,3,3,256,256]{4,3,2,1,0:T(8,128)}) %all-reduce.29.cloned.1.call-update) | async-done | bytes 7077904 | tf_op jit(solution)/shard_map/psum | solution.py:108
  283.2 2.0 copy.167
  285.2 0.9 copy.166
  286.1 0.9 copy.165
  287.1 1.8 convolution_bitcast_fusion.11
  288.8 3.5 collective-permute-start.11
  292.3 1.5 collective-permute-start.10
  295.5 1.7 convolution_bitcast_fusion.9
  297.1 1.6 convolution_bitcast_fusion.10
  298.8 1.1 fusion.72
  299.9 14.6 %collective-permute-done.11 = bf16[1,8,128,256]{3,2,1,0:T(8,128)(2,1)S(1)} collective-permute-done((bf16[1,8,128,256]{3,2,1,0:T(8,128)(2,1)S(1)}, bf16[1,8,128,256]{3,2,1,0:T(8,128)(2,1)S(1)}, u32[]{:S(2)}, u32[]{:S(2)}) %collective-permute-start.11) | collective-permute-done | bytes 524320 | tf_op jit(solution)/shard_map/ppermute | solution.py:11
  316.2 1.1 fusion.59
  317.3 1.2 fusion.57
  318.5 349.4 %all-reduce.31.cloned.1.call-done = f32[3,3,3,256,256]{4,3,2,1,0:T(8,128)} async-done(((f32[3,3,3,256,256]{4,3,2,1,0:T(8,128)}), f32[3,3,3,256,256]{4,3,2,1,0:T(8,128)}) %all-reduce.31.cloned.1.call-update) | async-done | bytes 7077904 | tf_op jit(solution)/shard_map/psum | solution.py:108
  667.9 6.7 copy.197
  (126 shorter events, 15.0 us)
Async XLA Ops:
  7.2 276.0 %all-reduce.29.cloned.1.call-start = ((), (), s32[]{:S(2)}) async-start(), calls=%async_computation | async-start | bytes 14155776 | tf_op jit(solution)/shard_map/psum | solution.py:108
  10.7 31.5 %collective-permute-start.1 = (bf16[1,8,128,256]{3,2,1,0:T(8,128)(2,1)}, bf16[1,8,128,256]{3,2,1,0:T(8,128)(2,1)}, u32[]{:S(2)}, u32[]{:S(2)}) collective-permute-start(bf16[1,8,128,256]{3,2,1,0:T(8,128)(2,1)} %fusion.33), channel_id=1, source_target_pairs={{16,0},{20,4},{24,8},{28,12},{32,16},{36,20},{40,24},{44,28},{48,3... | collective-permute-start | bytes 1572872 | tf_op jit(solution)/shard_map/ppermute | solution.py:11
  12.0 32.1 %collective-permute-start = (bf16[1,8,128,256]{3,2,1,0:T(8,128)(2,1)}, bf16[1,8,128,256]{3,2,1,0:T(8,128)(2,1)}, u32[]{:S(2)}, u32[]{:S(2)}) collective-permute-start(bf16[1,8,128,256]{3,2,1,0:T(8,128)(2,1)} %fusion.33), channel_id=1, source_target_pairs={{0,16},{4,20},{8,24},{12,28},{16,32},{20,36},{24,40},{28,44},{32,4... | collective-permute-start | bytes 1572872 | tf_op jit(solution)/shard_map/ppermute | solution.py:11
  17.4 40.2 %collective-permute-start.7 = (bf16[1,8,128,256]{3,2,1,0:T(8,128)(2,1)}, bf16[1,8,128,256]{3,2,1,0:T(8,128)(2,1)}, u32[]{:S(2)}, u32[]{:S(2)}) collective-permute-start(bf16[1,8,128,256]{3,2,1,0:T(8,128)(2,1)} %param.5), channel_id=1, source_target_pairs={{0,64},{4,68},{8,72},{12,76},{16,80},{20,84},{24,88},{28,92},{32,9... | collective-permute-start | bytes 1572872 | tf_op jit(solution)/shard_map/ppermute | solution.py:11
  24.4 35.0 %collective-permute-start.6 = (bf16[1,8,128,256]{3,2,1,0:T(8,128)(2,1)}, bf16[1,8,128,256]{3,2,1,0:T(8,128)(2,1)}, u32[]{:S(2)}, u32[]{:S(2)}) collective-permute-start(bf16[1,8,128,256]{3,2,1,0:T(8,128)(2,1)} %param.5), channel_id=1, source_target_pairs={{64,0},{68,4},{72,8},{76,12},{80,16},{84,20},{88,24},{92,28},{96,3... | collective-permute-start | bytes 1572872 | tf_op jit(solution)/shard_map/ppermute | solution.py:11
  29.2 0.9 copy-start.8
  30.1 1.9 copy-start.3
  30.1 1.9 copy-start.10
  32.0 4.8 copy-start.2
  36.8 1.6 copy-start.21
  38.3 1.5 copy-start.17
  38.3 2.4 copy-start.7
  38.4 2.6 copy-start.15
  38.4 3.6 copy-start.19
  45.7 1.0 copy-start
  45.7 1.4 copy-start.5
  45.7 1.7 copy-start.6
  49.2 8.4 %copy-start.14 = (bf16[1,1,3,256,256]{4,3,2,1,0:T(8,128)(2,1)S(1)}, bf16[1,1,3,256,256]{4,3,2,1,0:T(8,128)(2,1)}, u32[]{:S(2)}) copy-start(bf16[1,1,3,256,256]{4,3,2,1,0:T(8,128)(2,1)} %get-tuple-element.21) | copy-start | bytes 1179652
  49.6 9.7 %copy-start.22 = (bf16[1,8,128,256]{3,2,1,0:T(8,128)(2,1)}, bf16[1,8,128,256]{3,2,1,0:T(8,128)(2,1)S(1)}, u32[]{:S(2)}) copy-start(bf16[1,8,128,256]{3,2,1,0:T(8,128)(2,1)S(1)} %fusion.27) | copy-start | bytes 1572868
  49.6 16.5 %collective-permute-start.3 = (bf16[1,8,128,256]{3,2,1,0:T(8,128)(2,1)S(1)}, bf16[1,8,128,256]{3,2,1,0:T(8,128)(2,1)S(1)}, u32[]{:S(2)}, u32[]{:S(2)}) collective-permute-start(bf16[1,8,128,256]{3,2,1,0:T(8,128)(2,1)S(1)} %fusion.27), channel_id=1, source_target_pairs={{32,0},{36,4},{40,8},{44,12},{48,16},{52,20},{56,24},{60,28},{64,3... | collective-permute-start | bytes 1572872 | tf_op jit(solution)/shard_map/ppermute | solution.py:11
  50.9 27.4 %collective-permute-start.2 = (bf16[1,8,128,256]{3,2,1,0:T(8,128)(2,1)S(1)}, bf16[1,8,128,256]{3,2,1,0:T(8,128)(2,1)S(1)}, u32[]{:S(2)}, u32[]{:S(2)}) collective-permute-start(bf16[1,8,128,256]{3,2,1,0:T(8,128)(2,1)S(1)} %fusion.27), channel_id=1, source_target_pairs={{0,32},{4,36},{8,40},{12,44},{16,48},{20,52},{24,56},{28,60},{32,6... | collective-permute-start | bytes 1572872 | tf_op jit(solution)/shard_map/ppermute | solution.py:11
  59.3 1.0 copy-start.12
  59.4 6.7 copy-start.29
  66.1 0.9 copy-start.38
  66.7 11.6 %copy-start.28 = (bf16[1,1,3,256,256]{3,4,2,1,0:T(8,128)(2,1)S(1)}, bf16[1,1,3,256,256]{3,4,2,1,0:T(8,128)(2,1)}, u32[]{:S(2)}) copy-start(bf16[1,1,3,256,256]{3,4,2,1,0:T(8,128)(2,1)} %copy.163) | copy-start | bytes 1179652
  78.3 0.8 copy-start.36
  79.6 2.1 copy-start.4
  81.8 18.6 %copy-start.20 = (bf16[1,1,3,256,256]{4,3,2,1,0:T(8,128)(2,1)S(1)}, bf16[1,1,3,256,256]{4,3,2,1,0:T(8,128)(2,1)}, u32[]{:S(2)}) copy-start(bf16[1,1,3,256,256]{4,3,2,1,0:T(8,128)(2,1)} %get-tuple-element.17) | copy-start | bytes 1179652
  83.2 49.4 %collective-permute-start.5 = (bf16[1,8,128,256]{3,2,1,0:T(8,128)(2,1)}, bf16[1,8,128,256]{3,2,1,0:T(8,128)(2,1)}, u32[]{:S(2)}, u32[]{:S(2)}) collective-permute-start(bf16[1,8,128,256]{3,2,1,0:T(8,128)(2,1)} %get-tuple-element.47), channel_id=1, source_target_pairs={{64,0},{68,4},{72,8},{76,12},{80,16},{84,20},{88,24},{92,28},{96,3... | collective-permute-start | bytes 1572872 | tf_op jit(solution)/shard_map/ppermute | solution.py:11
  84.5 49.8 %collective-permute-start.4 = (bf16[1,8,128,256]{3,2,1,0:T(8,128)(2,1)}, bf16[1,8,128,256]{3,2,1,0:T(8,128)(2,1)}, u32[]{:S(2)}, u32[]{:S(2)}) collective-permute-start(bf16[1,8,128,256]{3,2,1,0:T(8,128)(2,1)} %get-tuple-element.47), channel_id=1, source_target_pairs={{0,64},{4,68},{8,72},{12,76},{16,80},{20,84},{24,88},{28,92},{32,9... | collective-permute-start | bytes 1572872 | tf_op jit(solution)/shard_map/ppermute | solution.py:11
  93.2 26.8 %collective-permute-start.9 = (bf16[1,8,128,256]{3,2,1,0:T(8,128)(2,1)S(1)}, bf16[1,8,128,256]{3,2,1,0:T(8,128)(2,1)}, u32[]{:S(2)}, u32[]{:S(2)}) collective-permute-start(bf16[1,8,128,256]{3,2,1,0:T(8,128)(2,1)S(1)} %get-tuple-element.46), channel_id=1, source_target_pairs={{0,32},{4,36},{8,40},{12,44},{16,48},{20,52},{24,56},{28,60},{32,6... | collective-permute-start | bytes 1572872 | tf_op jit(solution)/shard_map/ppermute | solution.py:11
  98.8 23.1 %collective-permute-start.8 = (bf16[1,8,128,256]{3,2,1,0:T(8,128)(2,1)S(1)}, bf16[1,8,128,256]{3,2,1,0:T(8,128)(2,1)}, u32[]{:S(2)}, u32[]{:S(2)}) collective-permute-start(bf16[1,8,128,256]{3,2,1,0:T(8,128)(2,1)S(1)} %get-tuple-element.46), channel_id=1, source_target_pairs={{32,0},{36,4},{40,8},{44,12},{48,16},{52,20},{56,24},{60,28},{64,3... | collective-permute-start | bytes 1572872 | tf_op jit(solution)/shard_map/ppermute | solution.py:11
  100.3 2.3 copy-start.24
  106.5 3.0 copy-start.23
  109.4 3.1 copy-start.27
  109.4 3.1 copy-start.39
  112.5 2.2 copy-start.1
  114.7 1.0 copy-start.37
  115.7 4.3 copy-start.18
  121.7 1.0 copy-start.16
  130.2 2.3 copy-start.25
  134.2 1.8 copy-start.34
  136.0 1.4 copy-start.26
  139.1 1.9 copy-start.32
  139.1 1.9 copy-start.33
  139.1 1.9 copy-start.35
  144.9 523.0 %all-reduce.31.cloned.1.call-start = ((), (), s32[]{:S(2)}) async-start(), calls=%async_computation.1 | async-start | bytes 14155776 | tf_op jit(solution)/shard_map/psum | solution.py:108
  283.2 2.0 copy-start.13
  283.2 2.9 copy-start.11
  286.1 7.7 %copy-start.9 = (bf16[1,1,3,256,256]{4,3,2,1,0:T(8,128)(2,1)S(1)}, bf16[1,1,3,256,256]{4,3,2,1,0:T(8,128)(2,1)}, u32[]{:S(2)}) copy-start(bf16[1,1,3,256,256]{4,3,2,1,0:T(8,128)(2,1)} %copy-done.8) | copy-start | bytes 1179652
  288.8 25.7 %collective-permute-start.11 = (bf16[1,8,128,256]{3,2,1,0:T(8,128)(2,1)S(1)}, bf16[1,8,128,256]{3,2,1,0:T(8,128)(2,1)S(1)}, u32[]{:S(2)}, u32[]{:S(2)}) collective-permute-start(bf16[1,8,128,256]{3,2,1,0:T(8,128)(2,1)S(1)} %fusion.47), channel_id=1, source_target_pairs={{0,16},{4,20},{8,24},{12,28},{16,32},{20,36},{24,40},{28,44},{32,4... | collective-permute-start | bytes 1572872 | tf_op jit(solution)/shard_map/ppermute | solution.py:11
  292.3 22.8 %collective-permute-start.10 = (bf16[1,8,128,256]{3,2,1,0:T(8,128)(2,1)S(1)}, bf16[1,8,128,256]{3,2,1,0:T(8,128)(2,1)S(1)}, u32[]{:S(2)}, u32[]{:S(2)}) collective-permute-start(bf16[1,8,128,256]{3,2,1,0:T(8,128)(2,1)S(1)} %fusion.47), channel_id=1, source_target_pairs={{16,0},{20,4},{24,8},{28,12},{32,16},{36,20},{40,24},{44,28},{48,3... | collective-permute-start | bytes 1572872 | tf_op jit(solution)/shard_map/ppermute | solution.py:11
  294.5 1.0 copy-start.31
  294.7 2.5 copy-start.30
Sparse Core Ops, SparseCore 0:
  145.0 138.1 all-reduce.28
  285.7 382.0 all-reduce.30
